TPU v7x, 32 devices: a whole 2x2x4 slice. The times are simulated.
32 devices in a mesh: dp: 8 (over z, y), sp: 4 (over x, core).
Axes of the slice: x: 2, y: 2, z: 4, core: 2. Of those that a mesh axis runs over, the one named last changes fastest.
Arguments:
- tokens: bfloat16 [16, 1024, 512], P('dp', 'sp'), may hold values from -6 to 6
- lengths: int32 [16], P('dp'), may hold values from 64 to 1024, as said below
- post_query: bfloat16 [512, 512], replicated, may hold values from -0.25 to 0.25
- post_key: bfloat16 [512, 512], replicated, may hold values from -0.25 to 0.25
- post_value: bfloat16 [512, 512], replicated, may hold values from -0.25 to 0.25
- post_out: bfloat16 [512, 512], replicated, may hold values from -1 to 1
- post_gate: bfloat16 [512, 1376], replicated, may hold values from -0.25 to 0.25
- post_up: bfloat16 [512, 1376], replicated, may hold values from -0.25 to 0.25
- post_down: bfloat16 [1376, 512], replicated, may hold values from -0.15625 to 0.15625
- post_attn_gain: float32 [512], replicated, may hold values from 0.5 to 1.5
- post_ffn_gain: float32 [512], replicated, may hold values from 0.5 to 1.5
- pre_query: bfloat16 [512, 512], replicated, may hold values from -0.25 to 0.25
- pre_key: bfloat16 [512, 512], replicated, may hold values from -0.25 to 0.25
- pre_value: bfloat16 [512, 512], replicated, may hold values from -0.25 to 0.25
- pre_out: bfloat16 [512, 512], replicated, may hold values from -1 to 1
- pre_gate: bfloat16 [512, 1376], replicated, may hold values from -0.25 to 0.25
- pre_up: bfloat16 [512, 1376], replicated, may hold values from -0.25 to 0.25
- pre_down: bfloat16 [1376, 512], replicated, may hold values from -0.15625 to 0.15625
- pre_attn_gain: float32 [512], replicated, may hold values from 0.5 to 1.5
- pre_ffn_gain: float32 [512], replicated, may hold values from 0.5 to 1.5
- out_grad: bfloat16 [16, 1024, 512], P('dp', 'sp'), may hold values from -6 to 6
Outputs:
- output: bfloat16 [16, 1024, 512], P('dp', 'sp')
- tokens_grad: bfloat16 [16, 1024, 512], P('dp', 'sp')
- grad_post_query: float32 [512, 512], replicated
- grad_post_key: float32 [512, 512], replicated
- grad_post_value: float32 [512, 512], replicated
- grad_post_out: float32 [512, 512], replicated
- grad_post_gate: float32 [512, 1376], replicated
- grad_post_up: float32 [512, 1376], replicated
- grad_post_down: float32 [1376, 512], replicated
- grad_post_attn_gain: float32 [512], replicated
- grad_post_ffn_gain: float32 [512], replicated
- grad_pre_query: float32 [512, 512], replicated
- grad_pre_key: float32 [512, 512], replicated
- grad_pre_value: float32 [512, 512], replicated
- grad_pre_out: float32 [512, 512], replicated
- grad_pre_gate: float32 [512, 1376], replicated
- grad_pre_up: float32 [512, 1376], replicated
- grad_pre_down: float32 [1376, 512], replicated
- grad_pre_attn_gain: float32 [512], replicated
- grad_pre_ffn_gain: float32 [512], replicated
Inputs may be any that keep to these rules, and one draw needn't show every extreme that they name: `lengths`: some slot has length exactly 1024 and some exactly 64.
All inputs are finite; a program needn't handle non-finite values.
Results may differ from a plain program's by a relative error of at most 0.024.
Values may be sent and summed in bfloat16 or wider, within the bound.
No kernel may reach another device: no remote copies, remote signals or barrier semaphores. Data moves between devices by JAX's collectives and lax.ppermute only.
A program may use at most 192 MiB of HBM per device.

v0:
```python
import jax
import jax.numpy as jnp
from jax import lax
from jax.sharding import PartitionSpec as P

HEADS = 8
HD = 64
SEQ = 1024
eps = 1e-06


def norm_rows(values, gain_vec):
    return values * lax.rsqrt(jnp.mean(values * values, axis=-1, keepdims=True) + eps) * gain_vec


def rotary_tables(start, row_count):
    half_dim = HD // 2
    inverse = 10000.0 ** (-jnp.arange(half_dim, dtype=jnp.float32) * 2.0 / HD)
    positions = (start + jnp.arange(row_count, dtype=jnp.int32)).astype(jnp.float32)
    angles = positions[:, None] * inverse[None, :]
    cosine = jnp.concatenate([jnp.cos(angles), jnp.cos(angles)], axis=-1)
    sine_table = jnp.concatenate([jnp.sin(angles), jnp.sin(angles)], axis=-1)
    return (cosine, sine_table)


def rotate(values, cosine, sine_table):
    half_dim = values.shape[-1] // 2
    turned = jnp.concatenate([-values[..., half_dim:], values[..., :half_dim]], axis=-1)
    return values * cosine[:, None, :] + turned * sine_table[:, None, :]


def rotate_back(grads, cosine, sine_table):
    half_dim = grads.shape[-1] // 2
    turned = grads * sine_table[:, None, :]
    backward = jnp.concatenate([turned[..., half_dim:], -turned[..., :half_dim]], axis=-1)
    return grads * cosine[:, None, :] + backward


def gated(gate_act, up_act):
    return jax.nn.silu(gate_act) * up_act


def slot_scores(queries, key_heads, length):
    scores = jnp.einsum(
        "qhd,khd->hqk", queries, key_heads, preferred_element_type=jnp.float32
    ) * HD ** (-0.5)
    row_index = jnp.arange(SEQ, dtype=jnp.int32)[:, None]
    col_index = jnp.arange(SEQ, dtype=jnp.int32)[None, :]
    allowed = (col_index <= row_index) & (col_index < length)
    return jnp.where(allowed[None], scores, -1000000000.0)


def attend_slot(pieces):
    queries, key_heads, value_heads, length = pieces
    scores = slot_scores(queries, key_heads, length)
    maxima = jnp.max(scores, axis=-1, keepdims=True)
    log_total = maxima + jnp.log(jnp.sum(jnp.exp(scores - maxima), axis=-1, keepdims=True))
    softmax_p = jnp.exp(scores - log_total)
    mixed_heads = jnp.einsum(
        "hqk,khd->qhd",
        softmax_p.astype(jnp.bfloat16),
        value_heads,
        preferred_element_type=jnp.float32,
    )
    return (mixed_heads.astype(jnp.bfloat16), log_total)


def attend_back(pieces):
    queries, key_heads, value_heads, log_total, grad_mixed, length = pieces
    softmax_p = jnp.exp(slot_scores(queries, key_heads, length) - log_total)
    grad_values = jnp.einsum(
        "hqk,qhd->khd",
        softmax_p.astype(jnp.bfloat16),
        grad_mixed,
        preferred_element_type=jnp.float32,
    )
    grad_probs = jnp.einsum(
        "qhd,khd->hqk", grad_mixed, value_heads, preferred_element_type=jnp.float32
    )
    row_delta = jnp.sum(softmax_p * grad_probs, axis=-1, keepdims=True)
    grad_scores = (softmax_p * (grad_probs - row_delta)).astype(jnp.bfloat16)
    grad_queries = jnp.einsum(
        "hqk,khd->qhd", grad_scores, key_heads, preferred_element_type=jnp.float32
    ) * HD ** (-0.5)
    grad_keys = jnp.einsum(
        "hqk,qhd->khd", grad_scores, queries, preferred_element_type=jnp.float32
    ) * HD ** (-0.5)
    return (
        grad_queries.astype(jnp.bfloat16),
        grad_keys.astype(jnp.bfloat16),
        grad_values.astype(jnp.bfloat16),
    )


def layer_forward(inputs, weights, lengths, post_norm, cosine, sine_table):
    w_query, w_key, w_value, w_out, w_gate, w_up, w_down, gain_att, gain_ffn = weights
    group = lax.axis_size("sp")
    slot_count, row_count, width = inputs.shape
    local_heads = HEADS // group
    full_rows = row_count * group
    if post_norm:
        entry_rows = inputs.astype(jnp.bfloat16)
    else:
        entry_rows = norm_rows(inputs, gain_att).astype(jnp.bfloat16)

    def rotated(weight):
        product = jnp.einsum("nsd,de->nse", entry_rows, weight, preferred_element_type=jnp.float32)
        turned = rotate(product.reshape(slot_count, row_count, HEADS, HD), cosine, sine_table)
        return turned.astype(jnp.bfloat16).reshape(slot_count, row_count, group, local_heads * HD)

    query_rows = rotated(w_query)
    key_rows = rotated(w_key)
    value_rows = jnp.einsum("nsd,de->nse", entry_rows, w_value, preferred_element_type=jnp.float32)
    value_rows = value_rows.astype(jnp.bfloat16).reshape(
        slot_count, row_count, group, local_heads * HD
    )
    query_heads, key_heads, value_heads = (
        lax.all_to_all(query_rows, "sp", split_axis=2, concat_axis=1, tiled=True),
        lax.all_to_all(key_rows, "sp", split_axis=2, concat_axis=1, tiled=True),
        lax.all_to_all(value_rows, "sp", split_axis=2, concat_axis=1, tiled=True),
    )

    def head_view(values):
        return values.reshape(slot_count, full_rows, local_heads, HD)

    query_heads = head_view(query_heads)
    key_heads = head_view(key_heads)
    value_heads = head_view(value_heads)
    mixed_heads, log_total = lax.map(attend_slot, (query_heads, key_heads, value_heads, lengths))
    mixed_rows = lax.all_to_all(
        mixed_heads.reshape(slot_count, full_rows, 1, local_heads * HD),
        "sp",
        split_axis=1,
        concat_axis=2,
        tiled=True,
    )
    mixed_rows = mixed_rows.reshape(slot_count, row_count, width)
    middle = inputs + jnp.einsum(
        "nsd,de->nse", mixed_rows, w_out, preferred_element_type=jnp.float32
    )
    if post_norm:
        state_rows = norm_rows(middle, gain_att)
        ffn_in = state_rows.astype(jnp.bfloat16)
    else:
        state_rows = middle
        ffn_in = norm_rows(middle, gain_ffn).astype(jnp.bfloat16)
    gate_act = jnp.einsum("nsd,df->nsf", ffn_in, w_gate, preferred_element_type=jnp.float32)
    up_act = jnp.einsum("nsd,df->nsf", ffn_in, w_up, preferred_element_type=jnp.float32)
    hidden = gated(gate_act, up_act).astype(jnp.bfloat16)
    result = state_rows + jnp.einsum(
        "nsf,fd->nsd", hidden, w_down, preferred_element_type=jnp.float32
    )
    saved = (
        inputs,
        entry_rows,
        query_heads,
        key_heads,
        value_heads,
        log_total,
        mixed_rows,
        middle,
        ffn_in,
        gate_act,
        up_act,
        hidden,
        result,
    )
    if post_norm:
        return (norm_rows(result, gain_ffn), saved)
    return (result, saved)


def layer_backward(grad_output, saved, weights, lengths, post_norm, cosine, sine_table):
    w_query, w_key, w_value, w_out, w_gate, w_up, w_down, gain_att, gain_ffn = weights
    (
        inputs,
        entry_rows,
        query_heads,
        key_heads,
        value_heads,
        log_total,
        mixed_rows,
        middle,
        ffn_in,
        gate_act,
        up_act,
        hidden,
        result,
    ) = saved
    group = lax.axis_size("sp")
    slot_count, row_count, width = inputs.shape
    local_heads = HEADS // group
    full_rows = row_count * group
    if post_norm:
        discard, pull_result = jax.vjp(norm_rows, result, gain_ffn)
        grad_result, grad_gain_ffn = pull_result(grad_output)
    else:
        grad_result = grad_output
    grad_down_in = grad_result.astype(jnp.bfloat16)
    grad_w_down = jnp.einsum(
        "nsf,nsd->fd", hidden, grad_down_in, preferred_element_type=jnp.float32
    )
    grad_hidden = jnp.einsum(
        "nsd,fd->nsf", grad_down_in, w_down, preferred_element_type=jnp.float32
    )
    discard, pull_glu = jax.vjp(gated, gate_act, up_act)
    grad_gate, grad_up = pull_glu(grad_hidden)
    grad_gate = grad_gate.astype(jnp.bfloat16)
    grad_up = grad_up.astype(jnp.bfloat16)
    grad_w_gate = jnp.einsum("nsd,nsf->df", ffn_in, grad_gate, preferred_element_type=jnp.float32)
    grad_w_up = jnp.einsum("nsd,nsf->df", ffn_in, grad_up, preferred_element_type=jnp.float32)
    grad_ffn_in = jnp.einsum("nsf,df->nsd", grad_gate, w_gate, preferred_element_type=jnp.float32)
    grad_ffn_in = grad_ffn_in + jnp.einsum(
        "nsf,df->nsd", grad_up, w_up, preferred_element_type=jnp.float32
    )
    if post_norm:
        discard, pull_middle = jax.vjp(norm_rows, middle, gain_att)
        grad_middle, grad_gain_att = pull_middle(grad_result + grad_ffn_in)
    else:
        discard, pull_middle = jax.vjp(norm_rows, middle, gain_ffn)
        grad_normed, grad_gain_ffn = pull_middle(grad_ffn_in)
        grad_middle = grad_result + grad_normed
    grad_attn = grad_middle.astype(jnp.bfloat16)
    grad_w_out = jnp.einsum(
        "nsd,nse->de", mixed_rows, grad_attn, preferred_element_type=jnp.float32
    )
    grad_mixed = jnp.einsum(
        "nse,de->nsd", grad_attn, w_out, preferred_element_type=jnp.float32
    ).astype(jnp.bfloat16)
    grad_mixed = lax.all_to_all(
        grad_mixed.reshape(slot_count, row_count, group, local_heads * HD),
        "sp",
        split_axis=2,
        concat_axis=1,
        tiled=True,
    )
    grad_mixed = grad_mixed.reshape(slot_count, full_rows, local_heads, HD)
    grad_queries, grad_keys, grad_values = lax.map(
        attend_back, (query_heads, key_heads, value_heads, log_total, grad_mixed, lengths)
    )

    def head_pack(values):
        return values.reshape(slot_count, full_rows, 1, local_heads * HD)

    grad_query_rows, grad_key_rows, grad_value_rows = (
        lax.all_to_all(head_pack(grad_queries), "sp", split_axis=1, concat_axis=2, tiled=True),
        lax.all_to_all(head_pack(grad_keys), "sp", split_axis=1, concat_axis=2, tiled=True),
        lax.all_to_all(head_pack(grad_values), "sp", split_axis=1, concat_axis=2, tiled=True),
    )

    def unrotate(values):
        grads = values.astype(jnp.float32).reshape(slot_count, row_count, HEADS, HD)
        return (
            rotate_back(grads, cosine, sine_table)
            .astype(jnp.bfloat16)
            .reshape(slot_count, row_count, width)
        )

    grad_query_pre = unrotate(grad_query_rows)
    grad_key_pre = unrotate(grad_key_rows)
    grad_value_pre = grad_value_rows.reshape(slot_count, row_count, width)
    grad_w_query = jnp.einsum(
        "nsd,nse->de", entry_rows, grad_query_pre, preferred_element_type=jnp.float32
    )
    grad_w_key = jnp.einsum(
        "nsd,nse->de", entry_rows, grad_key_pre, preferred_element_type=jnp.float32
    )
    grad_w_value = jnp.einsum(
        "nsd,nse->de", entry_rows, grad_value_pre, preferred_element_type=jnp.float32
    )
    grad_entry = jnp.einsum(
        "nse,de->nsd", grad_query_pre, w_query, preferred_element_type=jnp.float32
    )
    grad_entry = grad_entry + jnp.einsum(
        "nse,de->nsd", grad_key_pre, w_key, preferred_element_type=jnp.float32
    )
    grad_entry = grad_entry + jnp.einsum(
        "nse,de->nsd", grad_value_pre, w_value, preferred_element_type=jnp.float32
    )
    if post_norm:
        grad_inputs = grad_middle + grad_entry
    else:
        discard, pull_inputs = jax.vjp(norm_rows, inputs, gain_att)
        grad_normed_in, grad_gain_att = pull_inputs(grad_entry)
        grad_inputs = grad_middle + grad_normed_in
    return (
        grad_inputs,
        (
            grad_w_query,
            grad_w_key,
            grad_w_value,
            grad_w_out,
            grad_w_gate,
            grad_w_up,
            grad_w_down,
            grad_gain_att,
            grad_gain_ffn,
        ),
    )


def reduce_grads(grads):
    weights = tuple((grad.astype(jnp.bfloat16) for grad in grads[:7]))
    summed = lax.psum(weights, ("dp", "sp"))
    gains = lax.psum(grads[7:], ("dp", "sp"))
    return tuple((grad.astype(jnp.float32) for grad in summed)) + tuple(gains)


def body(
    tokens,
    lengths,
    post_query,
    post_key,
    post_value,
    post_out,
    post_gate,
    post_up,
    post_down,
    post_attn_gain,
    post_ffn_gain,
    pre_query,
    pre_key,
    pre_value,
    pre_out,
    pre_gate,
    pre_up,
    pre_down,
    pre_attn_gain,
    pre_ffn_gain,
    out_grad,
):
    slot_count, row_count, width = tokens.shape
    start = lax.axis_index("sp") * row_count
    cosine, sine_table = rotary_tables(start, row_count)
    layer_one = (
        post_query,
        post_key,
        post_value,
        post_out,
        post_gate,
        post_up,
        post_down,
        post_attn_gain,
        post_ffn_gain,
    )
    layer_two = (
        pre_query,
        pre_key,
        pre_value,
        pre_out,
        pre_gate,
        pre_up,
        pre_down,
        pre_attn_gain,
        pre_ffn_gain,
    )
    inputs_one = tokens.astype(jnp.float32)
    middle_state, saved_one = layer_forward(
        inputs_one, layer_one, lengths, True, cosine, sine_table
    )
    final_state, saved_two = layer_forward(
        middle_state, layer_two, lengths, False, cosine, sine_table
    )
    output = final_state.astype(jnp.bfloat16)
    positions = start + jnp.arange(row_count, dtype=jnp.int32)
    valid_rows = (positions[None, :] < lengths[:, None]).astype(jnp.float32)
    grad_final = out_grad.astype(jnp.float32) * valid_rows[:, :, None]
    grad_middle_state, grads_two = layer_backward(
        grad_final, saved_two, layer_two, lengths, False, cosine, sine_table
    )
    grad_tokens, grads_one = layer_backward(
        grad_middle_state, saved_one, layer_one, lengths, True, cosine, sine_table
    )
    grads_one = reduce_grads(grads_one)
    grads_two = reduce_grads(grads_two)
    tokens_grad = grad_tokens.astype(jnp.bfloat16)
    return (
        output,
        tokens_grad,
        grads_one[0],
        grads_one[1],
        grads_one[2],
        grads_one[3],
        grads_one[4],
        grads_one[5],
        grads_one[6],
        grads_one[7],
        grads_one[8],
        grads_two[0],
        grads_two[1],
        grads_two[2],
        grads_two[3],
        grads_two[4],
        grads_two[5],
        grads_two[6],
        grads_two[7],
        grads_two[8],
    )


def solution(mesh):
    in_specs = (
        P("dp", "sp", None),
        P("dp"),
        P(),
        P(),
        P(),
        P(),
        P(),
        P(),
        P(),
        P(),
        P(),
        P(),
        P(),
        P(),
        P(),
        P(),
        P(),
        P(),
        P(),
        P(),
        P("dp", "sp", None),
    )
    out_specs = (
        P("dp", "sp", None),
        P("dp", "sp", None),
        P(),
        P(),
        P(),
        P(),
        P(),
        P(),
        P(),
        P(),
        P(),
        P(),
        P(),
        P(),
        P(),
        P(),
        P(),
        P(),
        P(),
        P(),
    )
    return jax.shard_map(body, mesh=mesh, in_specs=in_specs, out_specs=out_specs, check_vma=False)
```

profile of v0, /device:TPU:0, one launch (start us, length us, event | category | flops | bytes accessed | tf_op | source)
XLA Modules:
  0.0 970.4 jit_solution(17261309546535177547)
XLA Ops:
  9.9 4.2 all-to-all-start
  19.5 4.1 all-to-all-done
  27.9 8.0 all-to-all-done.1
  51.6 17.7 %while.52 = (s32[]{:T(128)}, bf16[2,1024,2,64]{1,3,2,0:T(8,128)(2,1)}, f32[2,2,1024,1]{2,1,3,0:T(2,128)S(1)}, bf16[2,1024,2,64]{1,3,2,0:T(8,128)(2,1)}, s32[2]{0...) while((s32[]{:T(128)}, ...), condition=%wide.region_3.4_spmd, body=%wide.region_0.3_spmd.sunk | while | flops 562166784 | bytes 36769988 | solution.py:129
  71.6 12.7 %all_to_all.216 = bf16[2,1024,1,128]{3,0,2,1:T(2,128)(2,1)S(1)} all-to-all(bf16[2,1024,1,128]{3,0,2,1:T(2,128)(2,1)} %copy.321), channel_id=1, replica_groups=mesh['dp'=8,'sp'=4] {'sp'}, dimensions={1} | all-to-all | bytes 1048576 | tf_op jit(solution)/shard_map/all_to_all | solution.py:130
  98.1 4.1 all-to-all-start.4
  115.5 8.0 all-to-all-done.5
  123.5 3.6 all-to-all-start.6
  139.4 17.7 %while.53 = (s32[]{:T(128)}, bf16[2,1024,2,64]{1,3,2,0:T(8,128)(2,1)}, f32[2,2,1024,1]{2,1,3,0:T(2,128)S(1)}, bf16[2,1024,2,64]{1,3,2,0:T(8,128)(2,1)}, s32[2]{0...) while((s32[]{:T(128)}, ...), condition=%wide.region_10.11_spmd, body=%wide.region_7.10_spmd.sunk | while | flops 562166784 | bytes 36769988 | solution.py:129
  159.1 4.4 all-to-all-start.7
  163.5 4.1 fusion.136
  167.6 4.7 all-to-all-done.7
  189.1 4.5 all-to-all-start.8
  197.1 5.4 all-to-all-done.8
  209.4 28.9 %while.54 = (s32[]{:T(128)}, bf16[2,1024,2,64]{1,3,2,0:T(8,128)(2,1)}, bf16[2,1024,2,64]{1,3,2,0:T(8,128)(2,1)}, bf16[2,1024,2,64]{1,3,2,0:T(8,128)(2,1)}, bf16[...) while((s32[]{:T(128)}, ...), condition=%wide.region_15.16_spmd, body=%wide.region_13.15_spmd.sunk | while | flops 1376386048 | bytes 86572392 | solution.py:238
  240.3 3.6 all-to-all-start.10
  252.8 4.1 all-to-all-start.9
  265.8 4.1 all-to-all-start.11
  302.6 4.4 all-to-all-start.12
  311.6 4.2 all-to-all-done.12
  322.7 29.0 %while.55 = (s32[]{:T(128)}, bf16[2,1024,2,64]{1,3,2,0:T(8,128)(2,1)}, bf16[2,1024,2,64]{1,3,2,0:T(8,128)(2,1)}, bf16[2,1024,2,64]{1,3,2,0:T(8,128)(2,1)}, bf16[...) while((s32[]{:T(128)}, ...), condition=%wide.region_21.22_spmd, body=%wide.region_19.21_spmd.sunk | while | flops 1376386048 | bytes 86572392 | solution.py:238
  353.7 3.7 all-to-all-start.14
  405.5 42.8 %all-reduce = (f32[512]{0:T(512)}, f32[512]{0:T(512)}, f32[512]{0:T(512)}, f32[512]{0:T(512)}) all-reduce(f32[512]{0:T(512)S(1)} %get-tuple-element.339, f32[512]{0:T(512)S(1)} %get-tuple-element.334, f32[512]{0:T(512)S(1)} %get-tuple-element.336, f32[512]{0:T(512)S(1)} %copy-done.113), channel_id=1, replica_groups=mesh['dp'=8,'sp'=4] {'dp','sp'}, use_global_device_ids=true, to_apply=%region_30.31 | all-reduce | flops 2048 | bytes 16384 | tf_op jit(solution)/shard_map/psum | solution.py:305
  452.7 487.4 %all-reduce.4.cloned.1.call-done = (bf16[512,512]{0,1:T(8,128)(2,1)}, bf16[512,512]{0,1:T(8,128)(2,1)}, bf16[512,512]{0,1:T(8,128)(2,1)}, bf16[512,512]{1,0:T(8,...) async-done(((bf16[512,512]{0,1:T(8,128)(2,1)}, ...) | async-done | bytes 12648464 | tf_op jit(solution)/shard_map/psum | solution.py:304
  (536 shorter events, 331.3 us)
Async XLA Ops:
  7.2 172.5 %copy-start = (bf16[512,1376]{0,1:T(8,128)(2,1)S(1)}, bf16[512,1376]{0,1:T(8,128)(2,1)}, u32[]{:S(2)}) copy-start(bf16[512,1376]{0,1:T(8,128)(2,1)} %param.44) | copy-start | bytes 4227076
  9.9 13.7 %all-to-all-start = ((bf16[2,256,4,128]{3,1,0,2:T(8,128)(2,1)}), bf16[2,256,4,128]{3,1,0,2:T(8,128)(2,1)}, u32[]{:S(2)}, u32[]{:S(2)}) async-start(bf16[2,256,4,128]{3,1,0,2:T(8,128)(2,1)} %bitcast.512), calls=%async_computation | async-start | bytes 1048576 | tf_op jit(solution)/shard_map/all_to_all | solution.py:120
  16.9 88.8 %copy-start.12 = (f32[256,8,64]{0,2,1:T(8,128)}, f32[256,8,64]{0,2,1:T(8,128)S(1)}, u32[]{:S(2)}) copy-start(f32[256,8,64]{0,2,1:T(8,128)S(1)} %mul.485) | copy-start | bytes 1572868
  23.6 12.3 %all-to-all-start.1 = ((bf16[2,256,4,128]{1,3,0,2:T(8,128)(2,1)}), bf16[2,256,4,128]{1,3,0,2:T(8,128)(2,1)S(1)}, u32[]{:S(2)}, u32[]{:S(2)}) async-start(bf16[2,256,4,128]{1,3,0,2:T(8,128)(2,1)} %copy.315), calls=%async_computation.1 | async-start | bytes 1048576 | tf_op jit(solution)/shard_map/all_to_all | solution.py:118
  35.9 12.3 %all-to-all-start.2 = ((bf16[2,256,4,128]{1,3,0,2:T(8,128)(2,1)}), bf16[2,256,4,128]{1,3,0,2:T(8,128)(2,1)S(1)}, u32[]{:S(2)}, u32[]{:S(2)}) async-start(bf16[2,256,4,128]{1,3,0,2:T(8,128)(2,1)} %copy.319), calls=%async_computation.2 | async-start | bytes 1048576 | tf_op jit(solution)/shard_map/all_to_all | solution.py:119
  69.3 20.2 %copy-start.2 = (bf16[2,1024,2,64]{1,3,2,0:T(8,128)(2,1)}, bf16[2,1024,2,64]{1,3,2,0:T(8,128)(2,1)S(1)}, u32[]{:S(2)}) copy-start(bf16[2,1024,2,64]{1,3,2,0:T(8,128)(2,1)S(1)} %get-tuple-element.864) | copy-start | bytes 1572868
  69.3 20.2 %copy-start.8 = (bf16[2,1024,2,64]{1,3,2,0:T(8,128)(2,1)}, bf16[2,1024,2,64]{1,3,2,0:T(8,128)(2,1)S(1)}, u32[]{:S(2)}) copy-start(bf16[2,1024,2,64]{1,3,2,0:T(8,128)(2,1)S(1)} %get-tuple-element.866) | copy-start | bytes 1572868
  69.3 20.2 %copy-start.95 = (f32[2,2,1024,1]{2,1,3,0:T(2,128)}, f32[2,2,1024,1]{2,1,3,0:T(2,128)S(1)}, u32[]{:S(2)}) copy-start(f32[2,2,1024,1]{2,1,3,0:T(2,128)S(1)} %get-tuple-element.810) | copy-start | bytes 49156
  98.1 13.1 %all-to-all-start.4 = ((bf16[2,256,4,128]{3,1,0,2:T(8,128)(2,1)}), bf16[2,256,4,128]{3,1,0,2:T(8,128)(2,1)}, u32[]{:S(2)}, u32[]{:S(2)}) async-start(bf16[2,256,4,128]{3,1,0,2:T(8,128)(2,1)} %bitcast.625), calls=%async_computation.4 | async-start | bytes 1048576 | tf_op jit(solution)/shard_map/all_to_all | solution.py:120
  111.2 12.3 %all-to-all-start.5 = ((bf16[2,256,4,128]{1,3,0,2:T(8,128)(2,1)}), bf16[2,256,4,128]{1,3,0,2:T(8,128)(2,1)S(1)}, u32[]{:S(2)}, u32[]{:S(2)}) async-start(bf16[2,256,4,128]{1,3,0,2:T(8,128)(2,1)} %copy.328), calls=%async_computation.5 | async-start | bytes 1048576 | tf_op jit(solution)/shard_map/all_to_all | solution.py:118
  123.5 12.4 %all-to-all-start.6 = ((bf16[2,256,4,128]{1,3,0,2:T(8,128)(2,1)}), bf16[2,256,4,128]{1,3,0,2:T(8,128)(2,1)S(1)}, u32[]{:S(2)}, u32[]{:S(2)}) async-start(bf16[2,256,4,128]{1,3,0,2:T(8,128)(2,1)} %copy.332), calls=%async_computation.6 | async-start | bytes 1048576 | tf_op jit(solution)/shard_map/all_to_all | solution.py:119
  159.1 13.3 %all-to-all-start.7 = ((bf16[2,1024,1,128]{3,0,2,1:T(2,128)(2,1)}), bf16[2,1024,1,128]{3,0,2,1:T(2,128)(2,1)}, u32[]{:S(2)}, u32[]{:S(2)}) async-start(bf16[2,1024,1,128]{3,0,2,1:T(2,128)(2,1)} %copy.334), calls=%async_computation.7 | async-start | bytes 1048576 | tf_op jit(solution)/shard_map/all_to_all | solution.py:130
  189.1 13.4 %all-to-all-start.8 = ((bf16[2,256,4,128]{3,1,0,2:T(8,128)(2,1)}), bf16[2,256,4,128]{3,1,0,2:T(8,128)(2,1)}, u32[]{:S(2)}, u32[]{:S(2)}) async-start(bf16[2,256,4,128]{3,1,0,2:T(8,128)(2,1)} %bitcast.638), calls=%async_computation.8 | async-start | bytes 1048576 | tf_op jit(solution)/shard_map/all_to_all | solution.py:230
  240.3 12.4 %all-to-all-start.10 = ((bf16[2,1024,1,128]{3,0,2,1:T(2,128)(2,1)}), bf16[2,1024,1,128]{3,0,2,1:T(2,128)(2,1)S(1)}, u32[]{:S(2)}, u32[]{:S(2)}) async-start(bf16[2,1024,1,128]{3,0,2,1:T(2,128)(2,1)} %copy.344), calls=%async_computation.10 | async-start | bytes 1048576 | tf_op jit(solution)/shard_map/all_to_all | solution.py:247
  252.8 13.1 %all-to-all-start.9 = ((bf16[2,1024,1,128]{3,0,2,1:T(2,128)(2,1)}), bf16[2,1024,1,128]{3,0,2,1:T(2,128)(2,1)}, u32[]{:S(2)}, u32[]{:S(2)}) async-start(bf16[2,1024,1,128]{3,0,2,1:T(2,128)(2,1)} %copy.339), calls=%async_computation.9 | async-start | bytes 1048576 | tf_op jit(solution)/shard_map/all_to_all | solution.py:246
  265.8 14.7 %all-to-all-start.11 = ((bf16[2,1024,1,128]{3,0,2,1:T(2,128)(2,1)}), bf16[2,1024,1,128]{3,0,2,1:T(2,128)(2,1)}, u32[]{:S(2)}, u32[]{:S(2)}) async-start(bf16[2,1024,1,128]{3,0,2,1:T(2,128)(2,1)} %copy.349), calls=%async_computation.11 | async-start | bytes 1048576 | tf_op jit(solution)/shard_map/all_to_all | solution.py:248
  302.6 13.3 %all-to-all-start.12 = ((bf16[2,256,4,128]{3,1,0,2:T(8,128)(2,1)}), bf16[2,256,4,128]{3,1,0,2:T(8,128)(2,1)}, u32[]{:S(2)}, u32[]{:S(2)}) async-start(bf16[2,256,4,128]{3,1,0,2:T(8,128)(2,1)} %bitcast.630), calls=%async_computation.12 | async-start | bytes 1048576 | tf_op jit(solution)/shard_map/all_to_all | solution.py:230
  353.7 12.5 %all-to-all-start.14 = ((bf16[2,1024,1,128]{3,0,2,1:T(2,128)(2,1)}), bf16[2,1024,1,128]{3,0,2,1:T(2,128)(2,1)S(1)}, u32[]{:S(2)}, u32[]{:S(2)}) async-start(bf16[2,1024,1,128]{3,0,2,1:T(2,128)(2,1)} %copy.359), calls=%async_computation.14 | async-start | bytes 1048576 | tf_op jit(solution)/shard_map/all_to_all | solution.py:247
  366.2 12.3 %all-to-all-start.13 = ((bf16[2,1024,1,128]{3,0,2,1:T(2,128)(2,1)}), bf16[2,1024,1,128]{3,0,2,1:T(2,128)(2,1)S(1)}, u32[]{:S(2)}, u32[]{:S(2)}) async-start(bf16[2,1024,1,128]{3,0,2,1:T(2,128)(2,1)} %copy.354), calls=%async_computation.13 | async-start | bytes 1048576 | tf_op jit(solution)/shard_map/all_to_all | solution.py:246
  379.3 12.3 %all-to-all-start.15 = ((bf16[2,1024,1,128]{3,0,2,1:T(2,128)(2,1)}), bf16[2,1024,1,128]{3,0,2,1:T(2,128)(2,1)S(1)}, u32[]{:S(2)}, u32[]{:S(2)}) async-start(bf16[2,1024,1,128]{3,0,2,1:T(2,128)(2,1)} %copy.364), calls=%async_computation.15 | async-start | bytes 1048576 | tf_op jit(solution)/shard_map/all_to_all | solution.py:248
  382.8 557.3 %all-reduce.4.cloned.1.call-start = ((), (), s32[]{:S(2)}) async-start(), calls=%async_computation.16 | async-start | bytes 25296896 | tf_op jit(solution)/shard_map/psum | solution.py:304
  401.9 46.4 %copy-start.39 = (bf16[2,256,512]{1,2,0:T(8,128)(2,1)S(1)}, bf16[2,256,512]{1,2,0:T(8,128)(2,1)}, u32[]{:S(2)}) copy-start(bf16[2,256,512]{1,2,0:T(8,128)(2,1)} %copy-done.38) | copy-start | bytes 1572868
  405.5 45.9 %copy-start.44 = (bf16[512,512]{1,0:T(8,128)(2,1)S(1)}, bf16[512,512]{1,0:T(8,128)(2,1)}, u32[]{:S(2)}) copy-start(bf16[512,512]{1,0:T(8,128)(2,1)} %param.33) | copy-start | bytes 1572868
  405.5 45.9 %copy-start.49 = (bf16[2,256,512]{2,1,0:T(8,128)(2,1)S(1)}, bf16[2,256,512]{2,1,0:T(8,128)(2,1)}, u32[]{:S(2)}) copy-start(bf16[2,256,512]{2,1,0:T(8,128)(2,1)} %reshape.559) | copy-start | bytes 1572868
  (135 other events, 437.5 us)
Sparse Core Ops, SparseCore 0:
  400.8 539.2 all-reduce.3
where the time goes:
time: 982 us; the launch traced here: 970 us
  waiting for transfers between devices  536 us (55%)
  matrix products  129 us (13%)
  local copies, waits for them, and re-layouts  113 us (12%)
  other arithmetic  61.6 us (6%)
  starting transfers between devices  58.3 us (6%)
  blocking collectives  55.5 us (6%)
  between operations  15.9 us (2%)
    psum x1, waiting for transfers between devices, reduce_grads(): summed = lax.psum(weights, ('dp', 'sp'))  487 us
    psum x1, blocking collectives, reduce_grads(): gains = lax.psum(grads[7:], ('dp', 'sp'))  42.8 us
    unnamed x201, local copies, waits for them, and re-layouts  20.6 us
  transfers between devices with their start and end apart: 16, of which 14 were waited for; matrix products, arithmetic and copies ran while one was open for 9% of the time, Pallas kernels for 0%

commit v1 on v0

--- a/solution.py
+++ b/solution.py
@@ -301,7 +301,7 @@
 
 def reduce_grads(grads):
     weights = tuple((grad.astype(jnp.bfloat16) for grad in grads[:7]))
-    summed = lax.psum(weights, ("dp", "sp"))
+    summed = lax.psum(lax.psum(weights, "sp"), "dp")
     gains = lax.psum(grads[7:], ("dp", "sp"))
     return tuple((grad.astype(jnp.float32) for grad in summed)) + tuple(gains)
 

time: 982 us -> 1090 us (1.11)
  waiting for transfers between devices: 536 us -> 646 us
    psum x1 -> x2, waiting for transfers between devices: 487 us -> 597 us  [reduce_grads(): summed = lax.psum(lax.psum(weights, 'sp'), 'dp')]
  transfers between devices with their start and end apart: 16 -> 17, of which waited for: 14 -> 15; matrix products, arithmetic and copies ran while one was open for 9% -> 8% of each run, Pallas kernels for 0% -> 0%
where the time goes in v1:
time: 1090 us; the launch traced here: 1080 us
  waiting for transfers between devices  646 us (59%)
  matrix products  129 us (12%)
  local copies, waits for them, and re-layouts  113 us (10%)
  other arithmetic  61.6 us (6%)
  starting transfers between devices  58.4 us (5%)
  blocking collectives  55.9 us (5%)
  between operations  15.9 us (1%)
    psum x2, waiting for transfers between devices, reduce_grads(): summed = lax.psum(lax.psum(weights, 'sp'), 'dp')  597 us
    psum x1, blocking collectives, reduce_grads(): gains = lax.psum(grads[7:], ('dp', 'sp'))  43.1 us
  transfers between devices with their start and end apart: 17, of which 15 were waited for; matrix products, arithmetic and copies ran while one was open for 8% of the time, Pallas kernels for 0%

profile of v1, /device:TPU:0, one launch (start us, length us, event | category | flops | bytes accessed | tf_op | source)
XLA Modules:
  0.0 1080.4 jit_solution(571360266713948091)
XLA Ops:
  9.9 4.2 all-to-all-start
  19.5 4.1 all-to-all-done
  27.9 8.0 all-to-all-done.1
  51.6 17.7 %while.52 = (s32[]{:T(128)}, bf16[2,1024,2,64]{1,3,2,0:T(8,128)(2,1)}, f32[2,2,1024,1]{2,1,3,0:T(2,128)S(1)}, bf16[2,1024,2,64]{1,3,2,0:T(8,128)(2,1)}, s32[2]{0...) while((s32[]{:T(128)}, ...), condition=%wide.region_3.4_spmd, body=%wide.region_0.3_spmd.sunk | while | flops 562166784 | bytes 36769988 | solution.py:129
  71.6 12.7 %all_to_all.216 = bf16[2,1024,1,128]{3,0,2,1:T(2,128)(2,1)S(1)} all-to-all(bf16[2,1024,1,128]{3,0,2,1:T(2,128)(2,1)} %copy.321), channel_id=1, replica_groups=mesh['dp'=8,'sp'=4] {'sp'}, dimensions={1} | all-to-all | bytes 1048576 | tf_op jit(solution)/shard_map/all_to_all | solution.py:130
  98.1 4.1 all-to-all-start.4
  115.5 8.0 all-to-all-done.5
  123.5 3.6 all-to-all-start.6
  139.4 17.7 %while.53 = (s32[]{:T(128)}, bf16[2,1024,2,64]{1,3,2,0:T(8,128)(2,1)}, f32[2,2,1024,1]{2,1,3,0:T(2,128)S(1)}, bf16[2,1024,2,64]{1,3,2,0:T(8,128)(2,1)}, s32[2]{0...) while((s32[]{:T(128)}, ...), condition=%wide.region_10.11_spmd, body=%wide.region_7.10_spmd.sunk | while | flops 562166784 | bytes 36769988 | solution.py:129
  159.1 4.4 all-to-all-start.7
  163.5 4.1 fusion.136
  167.6 4.7 all-to-all-done.7
  189.1 4.5 all-to-all-start.8
  197.1 5.4 all-to-all-done.8
  209.4 28.9 %while.54 = (s32[]{:T(128)}, bf16[2,1024,2,64]{1,3,2,0:T(8,128)(2,1)}, bf16[2,1024,2,64]{1,3,2,0:T(8,128)(2,1)}, bf16[2,1024,2,64]{1,3,2,0:T(8,128)(2,1)}, bf16[...) while((s32[]{:T(128)}, ...), condition=%wide.region_15.16_spmd, body=%wide.region_13.15_spmd.sunk | while | flops 1376386048 | bytes 86572392 | solution.py:238
  252.8 4.2 all-to-all-start.9
  265.9 4.1 all-to-all-start.11
  302.6 4.4 all-to-all-start.12
  311.6 4.2 all-to-all-done.12
  322.8 29.0 %while.55 = (s32[]{:T(128)}, bf16[2,1024,2,64]{1,3,2,0:T(8,128)(2,1)}, bf16[2,1024,2,64]{1,3,2,0:T(8,128)(2,1)}, bf16[2,1024,2,64]{1,3,2,0:T(8,128)(2,1)}, bf16[...) while((s32[]{:T(128)}, ...), condition=%wide.region_21.22_spmd, body=%wide.region_19.21_spmd.sunk | while | flops 1376386048 | bytes 86572392 | solution.py:238
  353.7 3.7 all-to-all-start.14
  400.7 228.5 %all-reduce.8.cloned.1.call-done = (bf16[512,512]{0,1:T(8,128)(2,1)}, bf16[512,512]{0,1:T(8,128)(2,1)}, bf16[512,512]{0,1:T(8,128)(2,1)}, bf16[512,512]{1,0:T(8,...) async-done(((bf16[512,512]{0,1:T(8,128)(2,1)}, ...) | async-done | bytes 12648464 | tf_op jit(solution)/shard_map/psum | solution.py:304
  634.1 43.1 %all-reduce = (f32[512]{0:T(512)}, f32[512]{0:T(512)}, f32[512]{0:T(512)}, f32[512]{0:T(512)}) all-reduce(f32[512]{0:T(512)S(1)} %get-tuple-element.339, f32[512]{0:T(512)S(1)} %get-tuple-element.334, f32[512]{0:T(512)S(1)} %get-tuple-element.336, f32[512]{0:T(512)S(1)} %copy-done.113), channel_id=1, replica_groups=mesh['dp'=8,'sp'=4] {'dp','sp'}, use_global_device_ids=true, to_apply=%region_37.38 | all-reduce | flops 2048 | bytes 16384 | tf_op jit(solution)/shard_map/psum | solution.py:305
  681.5 368.5 %all-reduce.6.cloned.1.call-done = (bf16[512,512]{0,1:T(8,128)(2,1)}, bf16[512,512]{0,1:T(8,128)(2,1)}, bf16[512,512]{0,1:T(8,128)(2,1)}, bf16[512,512]{1,0:T(8,...) async-done(((bf16[512,512]{0,1:T(8,128)(2,1)}, ...) | async-done | bytes 12648464 | tf_op jit(solution)/shard_map/psum | solution.py:304
  (539 shorter events, 335.0 us)
Async XLA Ops:
  7.2 172.5 %copy-start = (bf16[512,1376]{0,1:T(8,128)(2,1)S(1)}, bf16[512,1376]{0,1:T(8,128)(2,1)}, u32[]{:S(2)}) copy-start(bf16[512,1376]{0,1:T(8,128)(2,1)} %param.44) | copy-start | bytes 4227076
  9.9 13.7 %all-to-all-start = ((bf16[2,256,4,128]{3,1,0,2:T(8,128)(2,1)}), bf16[2,256,4,128]{3,1,0,2:T(8,128)(2,1)}, u32[]{:S(2)}, u32[]{:S(2)}) async-start(bf16[2,256,4,128]{3,1,0,2:T(8,128)(2,1)} %bitcast.512), calls=%async_computation | async-start | bytes 1048576 | tf_op jit(solution)/shard_map/all_to_all | solution.py:120
  16.9 88.8 %copy-start.12 = (f32[256,8,64]{0,2,1:T(8,128)}, f32[256,8,64]{0,2,1:T(8,128)S(1)}, u32[]{:S(2)}) copy-start(f32[256,8,64]{0,2,1:T(8,128)S(1)} %mul.485) | copy-start | bytes 1572868
  23.6 12.3 %all-to-all-start.1 = ((bf16[2,256,4,128]{1,3,0,2:T(8,128)(2,1)}), bf16[2,256,4,128]{1,3,0,2:T(8,128)(2,1)S(1)}, u32[]{:S(2)}, u32[]{:S(2)}) async-start(bf16[2,256,4,128]{1,3,0,2:T(8,128)(2,1)} %copy.315), calls=%async_computation.1 | async-start | bytes 1048576 | tf_op jit(solution)/shard_map/all_to_all | solution.py:118
  35.9 12.3 %all-to-all-start.2 = ((bf16[2,256,4,128]{1,3,0,2:T(8,128)(2,1)}), bf16[2,256,4,128]{1,3,0,2:T(8,128)(2,1)S(1)}, u32[]{:S(2)}, u32[]{:S(2)}) async-start(bf16[2,256,4,128]{1,3,0,2:T(8,128)(2,1)} %copy.319), calls=%async_computation.2 | async-start | bytes 1048576 | tf_op jit(solution)/shard_map/all_to_all | solution.py:119
  69.3 20.2 %copy-start.8 = (bf16[2,1024,2,64]{1,3,2,0:T(8,128)(2,1)}, bf16[2,1024,2,64]{1,3,2,0:T(8,128)(2,1)S(1)}, u32[]{:S(2)}) copy-start(bf16[2,1024,2,64]{1,3,2,0:T(8,128)(2,1)S(1)} %get-tuple-element.908) | copy-start | bytes 1572868
  69.3 20.2 %copy-start.95 = (f32[2,2,1024,1]{2,1,3,0:T(2,128)}, f32[2,2,1024,1]{2,1,3,0:T(2,128)S(1)}, u32[]{:S(2)}) copy-start(f32[2,2,1024,1]{2,1,3,0:T(2,128)S(1)} %get-tuple-element.824) | copy-start | bytes 49156
  98.1 13.1 %all-to-all-start.4 = ((bf16[2,256,4,128]{3,1,0,2:T(8,128)(2,1)}), bf16[2,256,4,128]{3,1,0,2:T(8,128)(2,1)}, u32[]{:S(2)}, u32[]{:S(2)}) async-start(bf16[2,256,4,128]{3,1,0,2:T(8,128)(2,1)} %bitcast.625), calls=%async_computation.4 | async-start | bytes 1048576 | tf_op jit(solution)/shard_map/all_to_all | solution.py:120
  111.2 12.3 %all-to-all-start.5 = ((bf16[2,256,4,128]{1,3,0,2:T(8,128)(2,1)}), bf16[2,256,4,128]{1,3,0,2:T(8,128)(2,1)S(1)}, u32[]{:S(2)}, u32[]{:S(2)}) async-start(bf16[2,256,4,128]{1,3,0,2:T(8,128)(2,1)} %copy.328), calls=%async_computation.5 | async-start | bytes 1048576 | tf_op jit(solution)/shard_map/all_to_all | solution.py:118
  123.5 12.4 %all-to-all-start.6 = ((bf16[2,256,4,128]{1,3,0,2:T(8,128)(2,1)}), bf16[2,256,4,128]{1,3,0,2:T(8,128)(2,1)S(1)}, u32[]{:S(2)}, u32[]{:S(2)}) async-start(bf16[2,256,4,128]{1,3,0,2:T(8,128)(2,1)} %copy.332), calls=%async_computation.6 | async-start | bytes 1048576 | tf_op jit(solution)/shard_map/all_to_all | solution.py:119
  159.1 13.3 %all-to-all-start.7 = ((bf16[2,1024,1,128]{3,0,2,1:T(2,128)(2,1)}), bf16[2,1024,1,128]{3,0,2,1:T(2,128)(2,1)}, u32[]{:S(2)}, u32[]{:S(2)}) async-start(bf16[2,1024,1,128]{3,0,2,1:T(2,128)(2,1)} %copy.334), calls=%async_computation.7 | async-start | bytes 1048576 | tf_op jit(solution)/shard_map/all_to_all | solution.py:130
  189.1 13.4 %all-to-all-start.8 = ((bf16[2,256,4,128]{3,1,0,2:T(8,128)(2,1)}), bf16[2,256,4,128]{3,1,0,2:T(8,128)(2,1)}, u32[]{:S(2)}, u32[]{:S(2)}) async-start(bf16[2,256,4,128]{3,1,0,2:T(8,128)(2,1)} %bitcast.638), calls=%async_computation.8 | async-start | bytes 1048576 | tf_op jit(solution)/shard_map/all_to_all | solution.py:230
  240.3 12.4 %all-to-all-start.10 = ((bf16[2,1024,1,128]{3,0,2,1:T(2,128)(2,1)}), bf16[2,1024,1,128]{3,0,2,1:T(2,128)(2,1)S(1)}, u32[]{:S(2)}, u32[]{:S(2)}) async-start(bf16[2,1024,1,128]{3,0,2,1:T(2,128)(2,1)} %copy.344), calls=%async_computation.10 | async-start | bytes 1048576 | tf_op jit(solution)/shard_map/all_to_all | solution.py:247
  252.8 13.1 %all-to-all-start.9 = ((bf16[2,1024,1,128]{3,0,2,1:T(2,128)(2,1)}), bf16[2,1024,1,128]{3,0,2,1:T(2,128)(2,1)}, u32[]{:S(2)}, u32[]{:S(2)}) async-start(bf16[2,1024,1,128]{3,0,2,1:T(2,128)(2,1)} %copy.339), calls=%async_computation.9 | async-start | bytes 1048576 | tf_op jit(solution)/shard_map/all_to_all | solution.py:246
  265.9 14.7 %all-to-all-start.11 = ((bf16[2,1024,1,128]{3,0,2,1:T(2,128)(2,1)}), bf16[2,1024,1,128]{3,0,2,1:T(2,128)(2,1)}, u32[]{:S(2)}, u32[]{:S(2)}) async-start(bf16[2,1024,1,128]{3,0,2,1:T(2,128)(2,1)} %copy.349), calls=%async_computation.11 | async-start | bytes 1048576 | tf_op jit(solution)/shard_map/all_to_all | solution.py:248
  302.6 13.3 %all-to-all-start.12 = ((bf16[2,256,4,128]{3,1,0,2:T(8,128)(2,1)}), bf16[2,256,4,128]{3,1,0,2:T(8,128)(2,1)}, u32[]{:S(2)}, u32[]{:S(2)}) async-start(bf16[2,256,4,128]{3,1,0,2:T(8,128)(2,1)} %bitcast.630), calls=%async_computation.12 | async-start | bytes 1048576 | tf_op jit(solution)/shard_map/all_to_all | solution.py:230
  353.7 12.5 %all-to-all-start.14 = ((bf16[2,1024,1,128]{3,0,2,1:T(2,128)(2,1)}), bf16[2,1024,1,128]{3,0,2,1:T(2,128)(2,1)S(1)}, u32[]{:S(2)}, u32[]{:S(2)}) async-start(bf16[2,1024,1,128]{3,0,2,1:T(2,128)(2,1)} %copy.359), calls=%async_computation.14 | async-start | bytes 1048576 | tf_op jit(solution)/shard_map/all_to_all | solution.py:247
  366.3 12.3 %all-to-all-start.13 = ((bf16[2,1024,1,128]{3,0,2,1:T(2,128)(2,1)}), bf16[2,1024,1,128]{3,0,2,1:T(2,128)(2,1)S(1)}, u32[]{:S(2)}, u32[]{:S(2)}) async-start(bf16[2,1024,1,128]{3,0,2,1:T(2,128)(2,1)} %copy.354), calls=%async_computation.13 | async-start | bytes 1048576 | tf_op jit(solution)/shard_map/all_to_all | solution.py:246
  379.3 12.3 %all-to-all-start.15 = ((bf16[2,1024,1,128]{3,0,2,1:T(2,128)(2,1)}), bf16[2,1024,1,128]{3,0,2,1:T(2,128)(2,1)S(1)}, u32[]{:S(2)}, u32[]{:S(2)}) async-start(bf16[2,1024,1,128]{3,0,2,1:T(2,128)(2,1)} %copy.364), calls=%async_computation.15 | async-start | bytes 1048576 | tf_op jit(solution)/shard_map/all_to_all | solution.py:248
  382.8 246.4 %all-reduce.8.cloned.1.call-start = ((), (), s32[]{:S(2)}) async-start(), calls=%async_computation.17 | async-start | bytes 25296896 | tf_op jit(solution)/shard_map/psum | solution.py:304
  400.7 649.4 %all-reduce.6.cloned.1.call-start = ((), (), s32[]{:S(2)}) async-start(), calls=%async_computation.16 | async-start | bytes 25296896 | tf_op jit(solution)/shard_map/psum | solution.py:304
  630.4 46.8 %copy-start.37 = (bf16[2,256,512]{1,2,0:T(8,128)(2,1)S(1)}, bf16[2,256,512]{1,2,0:T(8,128)(2,1)}, u32[]{:S(2)}) copy-start(bf16[2,256,512]{1,2,0:T(8,128)(2,1)} %copy-done.36) | copy-start | bytes 1572868
  634.0 46.2 %copy-start.44 = (bf16[512,512]{1,0:T(8,128)(2,1)S(1)}, bf16[512,512]{1,0:T(8,128)(2,1)}, u32[]{:S(2)}) copy-start(bf16[512,512]{1,0:T(8,128)(2,1)} %param.33) | copy-start | bytes 1572868
  634.0 46.2 %copy-start.49 = (bf16[2,256,512]{2,1,0:T(8,128)(2,1)S(1)}, bf16[2,256,512]{2,1,0:T(8,128)(2,1)}, u32[]{:S(2)}) copy-start(bf16[2,256,512]{2,1,0:T(8,128)(2,1)} %reshape.559) | copy-start | bytes 1572868
  (136 other events, 457.7 us)
Sparse Core Ops, SparseCore 0:
  400.8 228.3 all-reduce.7
  635.6 414.3 all-reduce.5
